TPU v7x, 256 devices: a whole 4x4x8 slice. The times are simulated.
256 devices in a mesh: neur: 32 (over y, z_hi, core), tm: 8 (over x, z_lo).
Axes of the slice: x: 4, y: 4, z: 8 (z_hi: 4, z_lo: 2; z = z_hi * 2 + z_lo), core: 2. Of those that a mesh axis runs over, the one named last changes fastest.
Arguments:
- spikes: int32 [1024, 262144], P(None, ('neur', 'tm')), may hold values from 0 to 9
- held_in: int32 [262144], P(('neur', 'tm')), may hold values 0 or 1
- readin_weight: bfloat16 [262144, 1024], P(('neur', 'tm')), may hold values from -0.01171875 to 0.01171875
- qkv_weight: bfloat16 [1024, 3, 1024], P(None, None, 'tm'), may hold values from -0.1875 to 0.1875
- out_weight: bfloat16 [1024, 1024], P('tm'), may hold values from -0.1875 to 0.1875
- up_weight: bfloat16 [1024, 4096], P(None, 'tm'), may hold values from -0.1875 to 0.1875
- down_weight: bfloat16 [4096, 1024], P('tm'), may hold values from -0.09375 to 0.09375
- norm_gain: float32 [1024], replicated, may hold values from 0.25 to 1.75
- mlp_gain: float32 [1024], replicated, may hold values from 0.25 to 1.75
- final_gain: float32 [1024], replicated, may hold values from 0.25 to 1.75
- readout_weight: bfloat16 [262144, 1024], P(('neur', 'tm')), may hold values from -0.1875 to 0.1875
- readout_bias: float32 [262144], P(('neur', 'tm')), may hold values from -3 to 3
Outputs:
- latents: bfloat16 [1024, 1024], P('neur')
- neuron_bits: float32 [262144], P(('neur', 'tm'))
- bits_per_spike: float32 [], replicated
All inputs are finite; a program needn't handle non-finite values. No bound on the sum of `held_in` on one device may be relied on, other than what follows from the above.
Results may differ from a plain program's by a relative error of at most 0.006.
Values may be sent and summed in bfloat16 or wider, within the bound.
No kernel may reach another device: no remote copies, remote signals or barrier semaphores. Data moves between devices by JAX's collectives and lax.ppermute only.
A program may use at most 64 MiB of HBM per device.

v0:
```python
import math
import jax
import jax.numpy as jnp
from jax import lax
from jax.sharding import PartitionSpec as P

HEAD_DIM = 128


def normed(values, gain_vec):
    return values * lax.rsqrt(jnp.mean(values * values, -1, keepdims=True) + 1e-05) * gain_vec


def on_device(
    spikes,
    held_in,
    readin_weight,
    qkv_weight,
    out_weight,
    up_weight,
    down_weight,
    norm_gain,
    mlp_gain,
    final_gain,
    readout_weight,
    readout_bias,
):
    frames_all = spikes.shape[0]
    rows_here = frames_all // lax.axis_size("neur")
    masked = (spikes * held_in[None, :]).astype(jnp.bfloat16)
    heldout = (1 - held_in).astype(jnp.float32)
    counts = jnp.sum(spikes, 0).astype(jnp.float32)
    partial_sum = jnp.dot(masked, readin_weight, preferred_element_type=jnp.float32)
    summed = lax.psum(partial_sum, ("neur", "tm"))
    stream = lax.dynamic_slice_in_dim(summed, lax.axis_index("neur") * rows_here, rows_here, 0)
    model_dim = stream.shape[1]
    head_cols = qkv_weight.shape[2]
    local_heads = head_cols // HEAD_DIM
    attn_in = normed(stream, norm_gain).astype(jnp.bfloat16)
    projected = jnp.dot(
        attn_in, qkv_weight.reshape(model_dim, 3 * head_cols), preferred_element_type=jnp.float32
    ).astype(jnp.bfloat16)
    queries = projected[:, :head_cols].reshape(rows_here, local_heads, HEAD_DIM)
    keys_local = projected[:, head_cols : 2 * head_cols]
    values_local = projected[:, 2 * head_cols :]
    scaling = 1.0 / math.sqrt(HEAD_DIM)
    key_rows = lax.all_gather(keys_local, "neur", axis=0, tiled=True).reshape(
        -1, local_heads, HEAD_DIM
    )
    value_rows = lax.all_gather(values_local, "neur", axis=0, tiled=True).reshape(
        -1, local_heads, HEAD_DIM
    )
    scores = (
        jnp.einsum("qhd,khd->hqk", queries, key_rows, preferred_element_type=jnp.float32) * scaling
    )
    weights = jnp.exp(scores)
    numerator = jnp.einsum(
        "hqk,khd->qhd", weights.astype(jnp.bfloat16), value_rows, preferred_element_type=jnp.float32
    )
    denominator = jnp.sum(weights, -1).T
    numerator, denominator = (numerator, denominator)
    heads_out = (
        (numerator / denominator[:, :, None]).astype(jnp.bfloat16).reshape(rows_here, head_cols)
    )
    attn_part = jnp.dot(heads_out, out_weight, preferred_element_type=jnp.float32)
    mixed_state = stream + lax.psum(attn_part, "tm")
    mlp_in = normed(mixed_state, mlp_gain).astype(jnp.bfloat16)
    hidden_act = jax.nn.gelu(jnp.dot(mlp_in, up_weight, preferred_element_type=jnp.float32)).astype(
        jnp.bfloat16
    )
    mlp_part = jnp.dot(hidden_act, down_weight, preferred_element_type=jnp.float32)
    final_state = mixed_state + lax.psum(mlp_part, "tm")
    latents = normed(final_state, final_gain).astype(jnp.bfloat16)
    log_rate = (
        lax.dot_general(
            lax.all_gather(latents, "neur", axis=0, tiled=True),
            readout_weight,
            (((1,), (1,)), ((), ())),
            preferred_element_type=jnp.float32,
        )
        + readout_bias[None, :]
    )
    observed = spikes.astype(jnp.float32)
    model_ll = jnp.sum(observed * log_rate - jnp.exp(log_rate), 0)
    null_ll = counts * jnp.log((counts + 1.0) / frames_all) - (counts + 1.0)
    gained = heldout * (model_ll - null_ll)
    neuron_bits = gained / (math.log(2.0) * (counts + 1.0))
    score_sum, spike_sum = lax.psum((jnp.sum(gained), jnp.sum(heldout * counts)), ("neur", "tm"))
    bits_total = score_sum / (math.log(2.0) * (1.0 + spike_sum))
    return (latents, neuron_bits, bits_total)


def solution(mesh):
    in_specs = (
        P(None, ("neur", "tm")),
        P(("neur", "tm")),
        P(("neur", "tm"), None),
        P(None, None, "tm"),
        P("tm", None),
        P(None, "tm"),
        P("tm", None),
        P(),
        P(),
        P(),
        P(("neur", "tm"), None),
        P(("neur", "tm")),
    )
    out_specs = (P("neur", None), P(("neur", "tm")), P())
    return jax.shard_map(
        on_device, mesh=mesh, in_specs=in_specs, out_specs=out_specs, check_vma=False
    )
```

profile of v0, /device:TPU:1, one launch (start us, length us, event | category | flops | bytes accessed | tf_op | source)
XLA Modules:
  0.0 675.9 jit_solution(17022954513759164385)
XLA Ops:
  7.2 0.0 copy-start
  7.2 0.0 all-reduce.5.cloned.1.call-start
  7.2 1.5 copy-done
  8.8 6.5 fusion
  15.3 0.0 copy-start.2
  15.3 0.0 copy-start.1
  15.3 0.0 copy-start.5
  15.3 0.0 all-reduce.5.cloned.1.call-update
  15.3 0.0 copy-start.3
  15.3 0.0 all-reduce.7.cloned.1.call-start
  15.4 1.4 copy.15
  16.8 269.4 %all-reduce.5.cloned.1.call-done = f32[1024,1024]{1,0:T(8,128)} async-done(((f32[1024,1024]{1,0:T(8,128)}), f32[1024,1024]{1,0:T(8,128)}) %all-reduce.5.cloned.1.call-update) | async-done | bytes 4194320 | tf_op jit(solution)/shard_map/psum | solution.py:34
  286.2 1.0 multiply_reduce_fusion.2
  287.2 0.0 copy-done.2
  287.2 1.2 convolution_convert_fusion
  288.5 42.8 %all_gather.10 = bf16[1024,128]{1,0:T(8,128)(2,1)S(1)} all-gather(bf16[32,128]{1,0:T(8,128)(2,1)S(1)} %get-tuple-element.11), channel_id=1, replica_groups=mesh['neur'=32,'tm'=8] {'neur'}, dimensions={0}, use_global_device_ids=true | all-gather | bytes 270336 | tf_op jit(solution)/shard_map/all_gather | solution.py:47
  331.3 0.3 fusion.38
  331.6 42.1 %all_gather.9 = bf16[1024,128]{1,0:T(8,128)(2,1)S(1)} all-gather(bf16[32,128]{1,0:T(8,128)(2,1)S(1)} %get-tuple-element.12), channel_id=1, replica_groups=mesh['neur'=32,'tm'=8] {'neur'}, dimensions={0}, use_global_device_ids=true | all-gather | bytes 270336 | tf_op jit(solution)/shard_map/all_gather | solution.py:50
  373.7 0.0 copy-done.1
  373.7 0.0 copy-start.6
  373.7 0.9 fusion.6
  374.6 0.0 all-reduce.7.cloned.1.call-update
  374.6 0.0 all-reduce.9.cloned.1.call-start
  374.7 67.4 %all-reduce.7.cloned.1.call-done = f32[32,1024]{1,0:T(8,128)} async-done(((f32[32,1024]{1,0:T(8,128)}), f32[32,1024]{1,0:T(8,128)}) %all-reduce.7.cloned.1.call-update) | async-done | bytes 131088 | tf_op jit(solution)/shard_map/psum | solution.py:66
  442.1 1.1 multiply_reduce_fusion.1
  443.2 0.0 copy-done.5
  443.2 2.8 fusion.16
  446.0 0.0 all-reduce.9.cloned.1.call-update
  446.0 0.0 all-gather.2.cloned.1.call-start
  446.1 76.6 %all-reduce.9.cloned.1.call-done = f32[32,1024]{1,0:T(8,128)} async-done(((f32[32,1024]{1,0:T(8,128)}), f32[32,1024]{1,0:T(8,128)}) %all-reduce.9.cloned.1.call-update) | async-done | bytes 131088 | tf_op jit(solution)/shard_map/psum | solution.py:72
  522.6 1.0 multiply_reduce_fusion
  523.7 0.0 copy-done.3
  523.7 0.7 multiply_convert_fusion.2
  524.4 0.0 all-gather.2.cloned.1.call-update
  524.4 2.5 reduce_sum.77
  526.9 0.0 copy-start.4
  526.9 58.2 %all-gather.2.cloned.1.call-done = bf16[1024,1024]{1,0:T(8,128)(2,1)} async-done(((bf16[32,1024]{1,0:T(8,128)(2,1)}), bf16[1024,1024]{1,0:T(8,128)(2,1)}) %all-gather.2.cloned.1.call-update) | async-done | bytes 2097168 | tf_op jit(solution)/shard_map/all_gather | solution.py:76
  585.1 0.0 copy-done.6
  585.1 6.2 subtract_reduce_fusion
  591.3 0.0 copy-done.4
  591.3 1.3 multiply_reduce_fusion.3
  592.6 74.4 %all-reduce = (f32[]{:T(128)}, f32[]{:T(128)}) all-reduce(f32[]{:T(128)} %get-tuple-element.4, f32[]{:T(128)} %get-tuple-element.3), channel_id=1, replica_groups=mesh['neur'=32,'tm'=8] {'neur','tm'}, use_global_device_ids=true, to_apply=%region_10.0 | all-reduce | flops 2 | bytes 16 | tf_op jit(solution)/shard_map/psum | solution.py:88
  (4 shorter events, 0.0 us)
Async XLA Ops:
  7.2 1.6 copy-start
  7.2 279.0 %all-reduce.5.cloned.1.call-start = ((), (), s32[]{:S(2)}) async-start(), calls=%async_computation | async-start | bytes 8388608 | tf_op jit(solution)/shard_map/psum | solution.py:34
  15.3 271.9 %copy-start.2 = (f32[1024]{0:T(1024)S(1)}, f32[1024]{0:T(1024)}, u32[]{:S(2)}) copy-start(f32[1024]{0:T(1024)} %param.19) | copy-start | bytes 12292
  15.3 358.4 %copy-start.1 = (bf16[128,1024]{1,0:T(8,128)(2,1)S(1)}, bf16[128,1024]{1,0:T(8,128)(2,1)}, u32[]{:S(2)}) copy-start(bf16[128,1024]{1,0:T(8,128)(2,1)} %param.16) | copy-start | bytes 786436
  15.3 428.0 %copy-start.5 = (f32[1024]{0:T(1024)S(1)}, f32[1024]{0:T(1024)}, u32[]{:S(2)}) copy-start(f32[1024]{0:T(1024)} %param.20) | copy-start | bytes 12292
  15.3 508.4 %copy-start.3 = (f32[1024]{0:T(1024)S(1)}, f32[1024]{0:T(1024)}, u32[]{:S(2)}) copy-start(f32[1024]{0:T(1024)} %param.21) | copy-start | bytes 12292
  15.3 426.8 %all-reduce.7.cloned.1.call-start = ((), (), s32[]{:S(2)}) async-start(), calls=%async_computation.1 | async-start | bytes 262144 | tf_op jit(solution)/shard_map/psum | solution.py:66
  373.7 211.5 %copy-start.6 = (f32[1024]{0:T(1024)S(1)}, f32[1024]{0:T(1024)}, u32[]{:S(2)}) copy-start(f32[1024]{0:T(1024)} %param.23) | copy-start | bytes 12292
  374.6 148.0 %all-reduce.9.cloned.1.call-start = ((), (), s32[]{:S(2)}) async-start(), calls=%async_computation.2 | async-start | bytes 262144 | tf_op jit(solution)/shard_map/psum | solution.py:72
  446.0 139.1 %all-gather.2.cloned.1.call-start = ((), (), s32[]{:S(2)}) async-start(), calls=%async_computation.3 | async-start | bytes 2162688 | tf_op jit(solution)/shard_map/all_gather | solution.py:76
  526.9 64.4 %copy-start.4 = (s32[1024]{0:T(1024)S(1)}, s32[1024]{0:T(1024)}, u32[]{:S(2)}) copy-start(s32[1024]{0:T(1024)} %param.13) | copy-start | bytes 12292
Sparse Core Ops, SparseCore 0:
  15.4 270.7 all-reduce.4
  374.8 67.3 all-reduce.6
  446.2 76.4 all-reduce.8
  526.0 59.1 all-gather.1
where the time goes:
time: 676 us
  waiting for transfers between devices  472 us (70%)
  blocking collectives  159 us (24%)
  matrix products  18 us (3%)
  between operations  16.2 us (2%)
  other arithmetic  7.64 us (1%)
    psum x1, waiting for transfers between devices, on_device(): summed = lax.psum(partial_sum, ('neur', 'tm'))  269 us
    psum x1, waiting for transfers between devices, on_device(): final_state = mixed_state + lax.psum(mlp_part, 'tm')  76.6 us
    psum x1, blocking collectives, on_device(): lax.psum((jnp.sum(gained), jnp.sum(heldout * counts)), ('neur', 'tm'))  74.4 us
    psum x1, waiting for transfers between devices, on_device(): mixed_state = stream + lax.psum(attn_part, 'tm')  67.4 us
    all_gather x1, waiting for transfers between devices, on_device(): lax.all_gather(latents, 'neur', axis=0, tiled=True)  58.2 us
    all_gather x1, blocking collectives, on_device(): lax.all_gather(keys_local, 'neur', axis=0, tiled=True)  42.8 us
    all_gather x1, blocking collectives, on_device(): lax.all_gather(values_local, 'neur', axis=0, tiled=True)  42.1 us
  transfers between devices with their start and end apart: 4, of which 4 were waited for; matrix products, arithmetic and copies ran while one was open for 1% of the time, Pallas kernels for 0%

commit v1 on v0

--- a/solution.py
+++ b/solution.py
@@ -47,9 +47,9 @@
     key_rows = lax.all_gather(keys_local, "neur", axis=0, tiled=True).reshape(
         -1, local_heads, HEAD_DIM
     )
-    value_rows = lax.all_gather(values_local, "neur", axis=0, tiled=True).reshape(
-        -1, local_heads, HEAD_DIM
-    )
+    value_rows = jnp.concatenate(
+        lax.all_to_all(jnp.stack([values_local] * lax.axis_size("neur")), "neur", 0, 0), axis=0
+    ).reshape(-1, local_heads, HEAD_DIM)
     scores = (
         jnp.einsum("qhd,khd->hqk", queries, key_rows, preferred_element_type=jnp.float32) * scaling
     )

time: 676 us -> 646 us (0.956)
  blocking collectives: 159 us -> 120 us
  starting transfers between devices: 0.16 us -> 10.6 us
    all_gather x1 -> x0, blocking collectives: 42.1 us -> none  [on_device(): lax.all_gather(values_local, 'neur', axis=0, tiled=True)]
    all_to_all x0 -> x1, starting transfers between devices: none -> 10.4 us  [on_device(): lax.all_to_all(jnp.stack([values_local] * lax.axis_size('neur')), 'neur',...]
  transfers between devices with their start and end apart: 4 -> 5, of which waited for: 4 -> 4; matrix products, arithmetic and copies ran while one was open for 1% -> 1% of each run, Pallas kernels for 0% -> 0%
where the time goes in v1:
time: 646 us
  waiting for transfers between devices  470 us (73%)
  blocking collectives  120 us (19%)
  matrix products  18 us (3%)
  between operations  16.2 us (3%)
  starting transfers between devices  10.6 us (2%)
  other arithmetic  7.64 us (1%)
    psum x1, waiting for transfers between devices, on_device(): summed = lax.psum(partial_sum, ('neur', 'tm'))  269 us
    psum x1, waiting for transfers between devices, on_device(): final_state = mixed_state + lax.psum(mlp_part, 'tm')  76.6 us
    psum x1, blocking collectives, on_device(): lax.psum((jnp.sum(gained), jnp.sum(heldout * counts)), ('neur', 'tm'))  74.4 us
    psum x1, waiting for transfers between devices, on_device(): mixed_state = stream + lax.psum(attn_part, 'tm')  65.4 us
    all_gather x1, waiting for transfers between devices, on_device(): lax.all_gather(latents, 'neur', axis=0, tiled=True)  58.2 us
    all_gather x1, blocking collectives, on_device(): lax.all_gather(keys_local, 'neur', axis=0, tiled=True)  45.7 us
  transfers between devices with their start and end apart: 5, of which 4 were waited for; matrix products, arithmetic and copies ran while one was open for 1% of the time, Pallas kernels for 0%

profile of v1, /device:TPU:1, one launch (start us, length us, event | category | flops | bytes accessed | tf_op | source)
XLA Modules:
  0.0 645.9 jit_solution(1866164208887646817)
XLA Ops:
  7.2 0.0 copy-start
  7.2 0.0 all-reduce.5.cloned.1.call-start
  7.2 1.5 copy-done
  8.8 6.5 %fusion = f32[1024,1024]{1,0:T(8,128)} fusion(bf16[1024,1024]{1,0:T(8,128)(2,1)S(1)} %copy-done, s32[1024,1024]{1,0:T(8,128)} %param.12, s32[1024]{0:T(1024)} %param.13), kind=kOutput, calls=%fused_computation.2 | convolution fusion | flops 2149580800 | bytes 10489856 | tf_op jit(solution)/shard_map/dot_general | solution.py:33
  15.3 0.0 copy-start.2
  15.3 0.0 copy-start.1
  15.3 0.0 copy-start.5
  15.3 0.0 all-reduce.5.cloned.1.call-update
  15.3 0.0 copy-start.3
  15.3 1.4 copy.15
  16.8 269.4 %all-reduce.5.cloned.1.call-done = f32[1024,1024]{1,0:T(8,128)} async-done(((f32[1024,1024]{1,0:T(8,128)}), f32[1024,1024]{1,0:T(8,128)}) %all-reduce.5.cloned.1.call-update) | async-done | bytes 4194320 | tf_op jit(solution)/shard_map/psum | solution.py:34
  286.2 1.0 multiply_reduce_fusion.2
  287.2 0.0 copy-done.2
  287.2 1.2 convolution_convert_fusion
  288.5 0.7 stack.2
  289.2 10.4 %all-to-all-start = ((bf16[32,32,128]{2,1,0:T(8,128)(2,1)}), bf16[32,32,128]{2,1,0:T(8,128)(2,1)S(1)}, u32[]{:S(2)}, u32[]{:S(2)}) async-start(bf16[32,32,128]{2,1,0:T(8,128)(2,1)} %stack.2), calls=%async_computation | async-start | bytes 524288 | tf_op jit(solution)/shard_map/all_to_all | solution.py:51
  299.6 0.0 all-reduce.7.cloned.1.call-start
  299.7 45.7 %all_gather.6 = bf16[1024,128]{1,0:T(8,128)(2,1)S(1)} all-gather(bf16[32,128]{1,0:T(8,128)(2,1)S(1)} %get-tuple-element.11), channel_id=1, replica_groups=mesh['neur'=32,'tm'=8] {'neur'}, dimensions={0}, use_global_device_ids=true | all-gather | bytes 270336 | tf_op jit(solution)/shard_map/all_gather | solution.py:47
  345.4 0.3 fusion.38
  345.7 0.0 all-to-all-done
  345.7 0.0 copy-done.1
  345.7 0.0 copy-start.6
  345.7 1.0 fusion.6
  346.6 0.0 all-reduce.7.cloned.1.call-update
  346.7 0.0 all-reduce.9.cloned.1.call-start
  346.7 65.4 %all-reduce.7.cloned.1.call-done = f32[32,1024]{1,0:T(8,128)} async-done(((f32[32,1024]{1,0:T(8,128)}), f32[32,1024]{1,0:T(8,128)}) %all-reduce.7.cloned.1.call-update) | async-done | bytes 131088 | tf_op jit(solution)/shard_map/psum | solution.py:66
  412.1 1.1 multiply_reduce_fusion.1
  413.2 0.0 copy-done.5
  413.2 2.8 fusion.16
  416.0 0.0 all-reduce.9.cloned.1.call-update
  416.1 0.0 all-gather.2.cloned.1.call-start
  416.1 76.6 %all-reduce.9.cloned.1.call-done = f32[32,1024]{1,0:T(8,128)} async-done(((f32[32,1024]{1,0:T(8,128)}), f32[32,1024]{1,0:T(8,128)}) %all-reduce.9.cloned.1.call-update) | async-done | bytes 131088 | tf_op jit(solution)/shard_map/psum | solution.py:72
  492.7 1.0 multiply_reduce_fusion
  493.7 0.0 copy-done.3
  493.7 0.7 multiply_convert_fusion.2
  494.4 0.0 all-gather.2.cloned.1.call-update
  494.5 2.5 reduce_sum.77
  496.9 0.0 copy-start.4
  496.9 58.2 %all-gather.2.cloned.1.call-done = bf16[1024,1024]{1,0:T(8,128)(2,1)} async-done(((bf16[32,1024]{1,0:T(8,128)(2,1)}), bf16[1024,1024]{1,0:T(8,128)(2,1)}) %all-gather.2.cloned.1.call-update) | async-done | bytes 2097168 | tf_op jit(solution)/shard_map/all_gather | solution.py:76
  555.2 0.0 copy-done.6
  555.2 6.2 subtract_reduce_fusion
  561.4 0.0 copy-done.4
  561.4 1.3 multiply_reduce_fusion.3
  562.7 74.4 %all-reduce = (f32[]{:T(128)}, f32[]{:T(128)}) all-reduce(f32[]{:T(128)} %get-tuple-element.4, f32[]{:T(128)} %get-tuple-element.3), channel_id=1, replica_groups=mesh['neur'=32,'tm'=8] {'neur','tm'}, use_global_device_ids=true, to_apply=%region_10.0 | all-reduce | flops 2 | bytes 16 | tf_op jit(solution)/shard_map/psum | solution.py:88
  (4 shorter events, 0.0 us)
Async XLA Ops:
  7.2 1.6 copy-start
  7.2 279.0 %all-reduce.5.cloned.1.call-start = ((), (), s32[]{:S(2)}) async-start(), calls=%async_computation.1 | async-start | bytes 8388608 | tf_op jit(solution)/shard_map/psum | solution.py:34
  15.3 271.9 %copy-start.2 = (f32[1024]{0:T(1024)S(1)}, f32[1024]{0:T(1024)}, u32[]{:S(2)}) copy-start(f32[1024]{0:T(1024)} %param.19) | copy-start | bytes 12292
  15.3 330.4 %copy-start.1 = (bf16[128,1024]{1,0:T(8,128)(2,1)S(1)}, bf16[128,1024]{1,0:T(8,128)(2,1)}, u32[]{:S(2)}) copy-start(bf16[128,1024]{1,0:T(8,128)(2,1)} %param.16) | copy-start | bytes 786436
  15.3 398.0 %copy-start.5 = (f32[1024]{0:T(1024)S(1)}, f32[1024]{0:T(1024)}, u32[]{:S(2)}) copy-start(f32[1024]{0:T(1024)} %param.20) | copy-start | bytes 12292
  15.3 478.4 %copy-start.3 = (f32[1024]{0:T(1024)S(1)}, f32[1024]{0:T(1024)}, u32[]{:S(2)}) copy-start(f32[1024]{0:T(1024)} %param.21) | copy-start | bytes 12292
  289.2 56.5 %all-to-all-start = ((bf16[32,32,128]{2,1,0:T(8,128)(2,1)}), bf16[32,32,128]{2,1,0:T(8,128)(2,1)S(1)}, u32[]{:S(2)}, u32[]{:S(2)}) async-start(bf16[32,32,128]{2,1,0:T(8,128)(2,1)} %stack.2), calls=%async_computation | async-start | bytes 524288 | tf_op jit(solution)/shard_map/all_to_all | solution.py:51
  299.6 112.5 %all-reduce.7.cloned.1.call-start = ((), (), s32[]{:S(2)}) async-start(), calls=%async_computation.2 | async-start | bytes 262144 | tf_op jit(solution)/shard_map/psum | solution.py:66
  345.7 209.5 %copy-start.6 = (f32[1024]{0:T(1024)S(1)}, f32[1024]{0:T(1024)}, u32[]{:S(2)}) copy-start(f32[1024]{0:T(1024)} %param.23) | copy-start | bytes 12292
  346.7 146.0 %all-reduce.9.cloned.1.call-start = ((), (), s32[]{:S(2)}) async-start(), calls=%async_computation.3 | async-start | bytes 262144 | tf_op jit(solution)/shard_map/psum | solution.py:72
  416.1 139.1 %all-gather.2.cloned.1.call-start = ((), (), s32[]{:S(2)}) async-start(), calls=%async_computation.4 | async-start | bytes 2162688 | tf_op jit(solution)/shard_map/all_gather | solution.py:76
  496.9 64.4 %copy-start.4 = (s32[1024]{0:T(1024)S(1)}, s32[1024]{0:T(1024)}, u32[]{:S(2)}) copy-start(s32[1024]{0:T(1024)} %param.13) | copy-start | bytes 12292
Sparse Core Ops, SparseCore 0:
  15.4 270.7 all-reduce.4
  346.8 65.3 all-reduce.6
  416.2 76.4 all-reduce.8
  496.0 59.1 all-gather.1
